TPU v7x, 512 devices: a whole 4x8x8 slice. The times are simulated.
512 devices in a mesh: row: 32 (over x_lo, y, core), col: 16 (over z, x_hi).
Axes of the slice: x: 4 (x_hi: 2, x_lo: 2; x = x_hi * 2 + x_lo), y: 8, z: 8, core: 2. Of those that a mesh axis runs over, the one named last changes fastest.
Arguments:
- support: bfloat16 [131072, 4096], P(('row', 'col')), may hold values from -6 to 6
- targets: bfloat16 [1024, 4096], P('col'), may hold values from -6 to 6
- panels: float32 [2, 128, 131072], P(None, None, ('row', 'col')), may hold values from -0.21875 to 0.21875
- diag_inverses: float32 [2, 128, 128], replicated, may hold values from -1 to 1.5, as said below
Outputs:
- solved: float32 [1024, 131072], P('col', 'row')
Inputs may be any that keep to these rules, and one draw needn't show every extreme that they name: Each diag_inverses[k] is lower triangular.
All inputs are finite; a program needn't handle non-finite values.
Results may differ from a plain program's by a relative error of at most 0.0003.
Values may be sent and summed in bfloat16 or wider, within the bound.
A program may use at most 64 MiB of HBM per device.

v0:
```python
import math
import jax
import jax.numpy as jnp
from jax import lax
from jax.sharding import PartitionSpec as P


def spread(value, axis, root):
    mine = lax.axis_index(axis) == root
    return lax.psum(jnp.where(mine, value, jnp.zeros_like(value)), axis)


def solve_head(pivot_cols, inverse):
    return jnp.dot(
        pivot_cols, inverse.T, precision=lax.Precision.HIGHEST, preferred_element_type=jnp.float32
    )


def apply_panel(current, solved_head, panel_cols):
    return current - jnp.dot(
        solved_head, panel_cols, precision=lax.Precision.HIGHEST, preferred_element_type=jnp.float32
    )


def shards(support, targets, panels, diag_inverses):
    feature_width = support.shape[1]
    kernel_scale = 0.5 / math.sqrt(feature_width)
    pivot_width = diag_inverses.shape[1]
    row_pos = lax.axis_index("row")
    products = jnp.einsum(
        "tf,sf->ts",
        lax.all_gather(targets, "col", axis=0, tiled=True),
        support,
        preferred_element_type=jnp.float32,
    )
    strip_tile = jnp.exp(kernel_scale * products)
    grid_tile = lax.all_to_all(strip_tile, "col", split_axis=0, concat_axis=1, tiled=True)
    panel_grid = lax.all_gather(panels, "col", axis=2, tiled=True)
    for panel_num in range(2):
        pivot_cols = grid_tile[:, :pivot_width]
        solved_head = spread(solve_head(pivot_cols, diag_inverses[panel_num]), "row", panel_num)
        updated = apply_panel(grid_tile, solved_head, panel_grid[panel_num])
        new_head = jnp.where(
            row_pos == panel_num,
            solved_head,
            jnp.where(row_pos < panel_num, pivot_cols, updated[:, :pivot_width]),
        )
        grid_tile = updated.at[:, :pivot_width].set(new_head)
    return grid_tile


def solution(mesh):
    in_specs = (P(("row", "col"), None), P("col", None), P(None, None, ("row", "col")), P())
    out_specs = P("col", "row")
    return jax.shard_map(shards, mesh=mesh, in_specs=in_specs, out_specs=out_specs, check_vma=False)
```

profile of v0, /device:TPU:2, one launch (start us, length us, event | category | flops | bytes accessed | tf_op | source)
XLA Modules:
  0.0 432.9 jit_solution(4030041354875455081)
XLA Ops:
  6.5 0.0 copy-start
  6.5 0.0 all-gather.3.cloned.1.call-start
  6.5 0.7 all-gather.3.cloned.1.call-update
  7.3 0.0 all-gather.5.cloned.1.call-start
  7.3 0.7 all-gather.5.cloned.1.call-update
  8.0 148.2 %all-gather.3.cloned.1.call-done = bf16[1024,4096]{1,0:T(8,128)(2,1)} async-done(((bf16[64,4096]{1,0:T(8,128)(2,1)}), bf16[1024,4096]{1,0:T(8,128)(2,1)}) %all-gather.3.cloned.1.call-update) | async-done | bytes 8388624 | tf_op jit(solution)/shard_map/all_gather | solution.py:32
  156.2 0.0 copy-done
  156.2 6.7 %fusion = f32[1024,256]{1,0:T(8,128)} fusion(bf16[1024,4096]{1,0:T(8,128)(2,1)} %all-gather.3.cloned.1.call-done, bf16[256,4096]{1,0:T(8,128)(2,1)S(1)} %copy-done), kind=kOutput, calls=%fused_computation.5 | convolution fusion | flops 2147745792 | bytes 11534336 | tf_op jit(solution)/shard_map/tf,sf->ts/dot_general | solution.py:30
  162.9 0.0 copy-start.3
  162.9 5.3 %all-to-all-start = ((f32[16,64,256]{2,1,0:T(8,128)}), f32[16,64,256]{2,1,0:T(8,128)S(1)}, u32[]{:S(2)}, u32[]{:S(2)}) async-start(f32[16,64,256]{2,1,0:T(8,128)} %bitcast.25), calls=%async_computation | async-start | bytes 2097152 | tf_op jit(solution)/shard_map/all_to_all | solution.py:37
  168.2 0.6 compare_reduce_fusion
  168.8 33.1 %all-to-all-done = f32[16,64,256]{2,1,0:T(8,128)S(1)} async-done(((f32[16,64,256]{2,1,0:T(8,128)}), f32[16,64,256]{2,1,0:T(8,128)S(1)}, u32[]{:S(2)}, u32[]{:S(2)}) %all-to-all-start) | async-done | bytes 1048608 | tf_op jit(solution)/shard_map/all_to_all | solution.py:37
  201.9 0.0 copy-start.2
  201.9 1.0 copy-done.2
  202.9 1.3 copy.6
  204.2 0.0 copy-done.3
  204.2 0.2 convolution_select_fusion.1
  204.5 106.4 %psum.14 = f32[64,128]{1,0:T(8,128)S(1)} all-reduce(f32[64,128]{1,0:T(8,128)S(1)} %convolution_select_fusion.1), channel_id=1, replica_groups=mesh['row'=32,'col'=16] {'row'}, use_global_device_ids=true, to_apply=%region_0.1 | all-reduce | flops 8192 | bytes 65536 | tf_op jit(solution)/shard_map/psum | solution.py:10
  310.9 0.0 all-gather.5.cloned.1.call-done
  310.9 2.8 convolution_subtract_fusion.1
  313.7 0.6 constant_dynamic-update-slice_fusion
  314.4 0.0 copy-start.1
  314.4 1.0 copy-done.1
  315.3 0.2 convolution_select_fusion
  315.6 104.4 %psum.15 = f32[64,128]{1,0:T(8,128)S(1)} all-reduce(f32[64,128]{1,0:T(8,128)S(1)} %convolution_select_fusion), channel_id=1, replica_groups=mesh['row'=32,'col'=16] {'row'}, use_global_device_ids=true, to_apply=%region_2.3 | all-reduce | flops 8192 | bytes 65536 | tf_op jit(solution)/shard_map/psum | solution.py:10
  420.0 4.0 convolution_subtract_fusion
  424.1 2.0 select_dynamic-update-slice_fusion
Async XLA Ops:
  6.5 149.6 %copy-start = (bf16[256,4096]{1,0:T(8,128)(2,1)S(1)}, bf16[256,4096]{1,0:T(8,128)(2,1)}, u32[]{:S(2)}) copy-start(bf16[256,4096]{1,0:T(8,128)(2,1)} %param.8) | copy-start | bytes 6291460
  6.5 149.6 %all-gather.3.cloned.1.call-start = ((), (), s32[]{:S(2)}) async-start(), calls=%async_computation.1 | async-start | bytes 8912896 | tf_op jit(solution)/shard_map/all_gather | solution.py:32
  7.3 303.6 %all-gather.5.cloned.1.call-start = ((), (), s32[]{:S(2)}) async-start(), calls=%async_computation.2 | async-start | bytes 4456448 | tf_op jit(solution)/shard_map/all_gather | solution.py:38
  162.9 41.3 %copy-start.3 = (f32[2,128,128]{2,1,0:T(8,128)S(1)}, f32[2,128,128]{2,1,0:T(8,128)}, u32[]{:S(2)}) copy-start(f32[2,128,128]{2,1,0:T(8,128)} %param.11) | copy-start | bytes 393220
  162.9 39.0 %all-to-all-start = ((f32[16,64,256]{2,1,0:T(8,128)}), f32[16,64,256]{2,1,0:T(8,128)S(1)}, u32[]{:S(2)}, u32[]{:S(2)}) async-start(f32[16,64,256]{2,1,0:T(8,128)} %bitcast.25), calls=%async_computation | async-start | bytes 2097152 | tf_op jit(solution)/shard_map/all_to_all | solution.py:37
  201.9 1.0 copy-start.2
  314.4 1.0 copy-start.1
Sparse Core Ops, SparseCore 0:
  10.5 145.5 all-gather.2
  159.2 117.2 all-gather.4
where the time goes:
time: 433 us
  blocking collectives  211 us (49%)
  waiting for transfers between devices  183 us (42%)
  matrix products  14.1 us (3%)
  between operations  13.5 us (3%)
  starting transfers between devices  5.33 us (1%)
    psum x2, blocking collectives, spread(): return lax.psum(jnp.where(mine, value, jnp.zeros_like(value)), axis)  211 us
    all_gather x1, waiting for transfers between devices, shards(): lax.all_gather(targets, 'col', axis=0, tiled=True)  148 us
    all_to_all x1, waiting for transfers between devices, shards(): lax.all_to_all(strip_tile, 'col', split_axis=0, concat_axis=1, tiled=True)  33.1 us
  transfers between devices with their start and end apart: 3, of which 2 were waited for; matrix products, arithmetic and copies ran while one was open for 2% of the time, Pallas kernels for 0%

commit v1 on v0

--- a/solution.py
+++ b/solution.py
@@ -7,7 +7,7 @@
 
 def spread(value, axis, root):
     mine = lax.axis_index(axis) == root
-    return lax.psum(jnp.where(mine, value, jnp.zeros_like(value)), axis)
+    return jnp.sum(lax.all_gather(jnp.where(mine, value, jnp.zeros_like(value)), axis), axis=0)
 
 
 def solve_head(pivot_cols, inverse):

time: 433 us -> 461 us (1.065)
  the two profiles are of different devices: /device:TPU:2 before, /device:TPU:1 now
where the time goes in v1:
time: 461 us; the launch traced here: 460 us
  waiting for transfers between devices  418 us (91%)
  matrix products  15.3 us (3%)
  between operations  13.2 us (3%)
  other arithmetic  5.91 us (1%)
    all_gather x1, waiting for transfers between devices, shards(): lax.all_gather(targets, 'col', axis=0, tiled=True)  150 us
    all_gather x2, waiting for transfers between devices, spread(): lax.all_gather(jnp.where(mine, value, jnp.zeros_like(value)), axis)  131 us
    all_gather x1, waiting for transfers between devices, shards(): panel_grid = lax.all_gather(panels, 'col', axis=2, tiled=True)  110 us
    all_to_all x1, waiting for transfers between devices, shards(): lax.all_to_all(strip_tile, 'col', split_axis=0, concat_axis=1, tiled=True)  26.2 us
  transfers between devices with their start and end apart: 5, of which 5 were waited for; matrix products, arithmetic and copies ran while one was open for 0% of the time, Pallas kernels for 0%

profile of v1, /device:TPU:1, one launch (start us, length us, event | category | flops | bytes accessed | tf_op | source)
XLA Modules:
  0.0 460.3 jit_solution(15037276233325081900)
XLA Ops:
  6.5 0.0 copy-start
  6.5 0.0 all-gather.7.cloned.1.call-start
  6.5 0.7 all-gather.7.cloned.1.call-update
  7.3 150.2 %all-gather.7.cloned.1.call-done = bf16[1024,4096]{1,0:T(8,128)(2,1)} async-done(((bf16[64,4096]{1,0:T(8,128)(2,1)}), bf16[1024,4096]{1,0:T(8,128)(2,1)}) %all-gather.7.cloned.1.call-update) | async-done | bytes 8388624 | tf_op jit(solution)/shard_map/all_gather | solution.py:32
  157.5 0.0 copy-done
  157.5 6.7 %fusion = f32[1024,256]{1,0:T(8,128)} fusion(bf16[1024,4096]{1,0:T(8,128)(2,1)} %all-gather.7.cloned.1.call-done, bf16[256,4096]{1,0:T(8,128)(2,1)S(1)} %copy-done), kind=kOutput, calls=%fused_computation.5 | convolution fusion | flops 2147745792 | bytes 11534336 | tf_op jit(solution)/shard_map/tf,sf->ts/dot_general | solution.py:30
  164.2 0.0 copy-start.3
  164.2 4.1 all-to-all-start
  168.4 0.0 all-gather.11.cloned.1.call-start
  168.4 26.2 %all-to-all-done = f32[16,64,256]{2,1,0:T(8,128)S(1)} async-done(((f32[16,64,256]{2,1,0:T(8,128)}), f32[16,64,256]{2,1,0:T(8,128)S(1)}, u32[]{:S(2)}, u32[]{:S(2)}) %all-to-all-start) | async-done | bytes 1048608 | tf_op jit(solution)/shard_map/all_to_all | solution.py:37
  194.6 0.0 copy-start.2
  194.6 1.0 copy-done.2
  195.6 1.3 copy.6
  196.9 0.0 copy-done.3
  196.9 0.9 convolution_select_fusion.1
  197.8 0.0 all-gather.11.cloned.1.call-update
  197.8 0.0 all-gather.9.cloned.1.call-start
  197.9 0.7 all-gather.9.cloned.1.call-update
  198.6 0.0 all-gather.13.cloned.1.call-start
  198.6 0.7 compare_reduce_fusion
  199.3 64.6 %all-gather.11.cloned.1.call-done = f32[2048,128]{1,0:T(8,128)} async-done(((f32[64,128]{1,0:T(8,128)}), f32[2048,128]{1,0:T(8,128)}) %all-gather.11.cloned.1.call-update) | async-done | bytes 1048592 | tf_op jit(solution)/shard_map/all_gather | solution.py:10
  263.8 1.3 reduce_sum.18
  265.1 109.6 %all-gather.9.cloned.1.call-done = f32[2,128,4096]{2,1,0:T(8,128)} async-done(((f32[2,128,256]{2,1,0:T(8,128)}), f32[2,128,4096]{2,1,0:T(8,128)}) %all-gather.9.cloned.1.call-update) | async-done | bytes 4194320 | tf_op jit(solution)/shard_map/all_gather | solution.py:38
  374.7 2.8 convolution_subtract_fusion.1
  377.5 0.6 constant_dynamic-update-slice_fusion
  378.2 0.0 copy-start.1
  378.2 1.0 copy-done.1
  379.2 0.9 convolution_select_fusion
  380.0 0.0 all-gather.13.cloned.1.call-update
  380.1 66.3 %all-gather.13.cloned.1.call-done = f32[2048,128]{1,0:T(8,128)} async-done(((f32[64,128]{1,0:T(8,128)}), f32[2048,128]{1,0:T(8,128)}) %all-gather.13.cloned.1.call-update) | async-done | bytes 1048592 | tf_op jit(solution)/shard_map/all_gather | solution.py:10
  446.4 1.3 reduce_sum.19
  447.7 4.0 convolution_subtract_fusion
  451.7 2.0 select_dynamic-update-slice_fusion
Async XLA Ops:
  6.5 151.0 %copy-start = (bf16[256,4096]{1,0:T(8,128)(2,1)S(1)}, bf16[256,4096]{1,0:T(8,128)(2,1)}, u32[]{:S(2)}) copy-start(bf16[256,4096]{1,0:T(8,128)(2,1)} %param.8) | copy-start | bytes 6291460
  6.5 151.0 %all-gather.7.cloned.1.call-start = ((), (), s32[]{:S(2)}) async-start(), calls=%async_computation.1 | async-start | bytes 8912896 | tf_op jit(solution)/shard_map/all_gather | solution.py:32
  164.2 32.7 %copy-start.3 = (f32[2,128,128]{2,1,0:T(8,128)S(1)}, f32[2,128,128]{2,1,0:T(8,128)}, u32[]{:S(2)}) copy-start(f32[2,128,128]{2,1,0:T(8,128)} %param.11) | copy-start | bytes 393220
  164.2 30.4 %all-to-all-start = ((f32[16,64,256]{2,1,0:T(8,128)}), f32[16,64,256]{2,1,0:T(8,128)S(1)}, u32[]{:S(2)}, u32[]{:S(2)}) async-start(f32[16,64,256]{2,1,0:T(8,128)} %bitcast.28), calls=%async_computation | async-start | bytes 2097152 | tf_op jit(solution)/shard_map/all_to_all | solution.py:37
  168.4 95.5 %all-gather.11.cloned.1.call-start = ((), (), s32[]{:S(2)}) async-start(), calls=%async_computation.3 | async-start | bytes 1081344 | tf_op jit(solution)/shard_map/all_gather | solution.py:10
  194.6 1.0 copy-start.2
  197.8 176.9 %all-gather.9.cloned.1.call-start = ((), (), s32[]{:S(2)}) async-start(), calls=%async_computation.2 | async-start | bytes 4456448 | tf_op jit(solution)/shard_map/all_gather | solution.py:38
  198.6 247.8 %all-gather.13.cloned.1.call-start = ((), (), s32[]{:S(2)}) async-start(), calls=%async_computation.4 | async-start | bytes 1081344 | tf_op jit(solution)/shard_map/all_gather | solution.py:10
  378.2 1.0 copy-start.1
Sparse Core Ops, SparseCore 0:
  10.5 146.9 all-gather.6
  197.9 65.8 all-gather.10
  266.9 107.7 all-gather.8
  380.2 66.1 all-gather.12
